TPU v7x, 128 devices: a whole 4x4x4 slice. The times are simulated.
128 devices in a mesh: space: 32 (over y, x, core), probe: 4 (over z).
Axes of the slice: x: 4, y: 4, z: 4, core: 2. Of those that a mesh axis runs over, the one named last changes fastest.
Arguments:
- points: float32 [1024, 3, 512], P('space')
- probes: float32 [1024, 32, 512], P('space', 'probe'), may hold values from -6 to 6
- counts: int32 [1024], P('space'), may hold values from 128 to 512, as said below
- near_list: int32 [1024, 8], P('space'), may hold values from 0 to 1023, as said below
- far_list: int32 [1024, 32], P('space'), may hold values from 0 to 1023, as said below
- coarse_list: int32 [56, 16], replicated, may hold values from 0 to 31, as said below
- leaf_proxy: float32 [1024, 3, 64], P('space')
- box_proxy: float32 [56, 3, 64], replicated
Outputs:
- result: float32 [1024, 32, 512], P('space', 'probe')
Inputs may be any that keep to these rules, and one draw needn't show every extreme that they name: `counts`: the first leaf of every block of 32 is full. `near_list`: entry 0 of row i is i; every entry lies within 32 of its row's index. `far_list`: every entry lies within 32 of its row's index. `coarse_list`: rows 0 to 31 belong to device boxes, the next 16 to pair boxes, the last 8 to quad boxes; each entry is a box index within its row's level and never the row's own box.
All inputs are finite; a program needn't handle non-finite values.
Results may differ from a plain program's by a relative error of at most 0.00018.
Values sent between devices are 32-bit elements; how exact they have to be, the bound alone decides.
No kernel may reach another device: no remote copies, remote signals or barrier semaphores. Data moves between devices by JAX's collectives and lax.ppermute only.
A program may use at most 64 MiB of HBM per device.

v0:
```python
import functools

import jax
import jax.numpy as jnp
from jax import lax
from jax.experimental import pallas as pl
from jax.experimental.pallas import tpu as pltpu
from jax.sharding import PartitionSpec as P

F32 = jnp.float32
BF16 = jnp.bfloat16
LOG2E = 1.4426950408889634
LN2 = 0.6931471805599453
SCALE = LOG2E * 1.7320508075688772 / 2.0
SLOPE = 0.5 / (LOG2E * LOG2E)
TINY = 1e-30
FEATURES = 48
UNITS = 8
ACROSS = False
COPIES = 8
CN = (((0,), (0,)), ((), ()))
NT = (((1,), (1,)), ((), ()))
NN = (((1,), (0,)), ((), ()))


def dot(left, right, dims):
    return lax.dot_general(left, right, dims, preferred_element_type=F32)


def split(value):
    high = value.astype(BF16)
    return high, (value - high.astype(F32)).astype(BF16)


def stacked(value):
    high = value.astype(BF16).astype(F32)
    return jnp.concatenate([high, value - high], axis=0).astype(BF16)


def exact_dot(left, right, dims):
    rows = left.shape[0]
    high, low = split(right)
    both = stacked(left)
    total = dot(both, high, dims) + dot(both, low, dims)
    return total[:rows] + total[rows:]


def small_dot(small, panel):
    high, low = split(panel)
    both = stacked(small)
    return dot(high, both, NT) + dot(low, both, NT)


def joined(columns):
    rows = columns.T
    return rows[0:8] + rows[8:16]


def slope_of(u):
    u = jnp.maximum(u, TINY)
    return u * jnp.exp2(-(u * lax.rsqrt(u)))


def value_of(u):
    u = jnp.maximum(u, TINY)
    w = u * lax.rsqrt(u)
    return (1.0 + LN2 * w) * jnp.exp2(-w)


def pieces(value):
    high = value.astype(BF16).astype(F32)
    rest = value - high
    middle = rest.astype(BF16).astype(F32)
    return high, middle, rest - middle


def features(rows, center, source, target):
    row = lax.broadcasted_iota(jnp.int32, rows.shape, 0)
    scaled = jnp.where(row < 3, (rows - center) * SCALE, 0.0)
    norm = jnp.sum(scaled * scaled, axis=0, keepdims=True)
    out = []
    if source:
        h, m, l = pieces(jnp.where(row == 3, norm, jnp.where(row == 4, 1.0, scaled)))
        out.append(jnp.concatenate([h, h, m, h, l, m], axis=0))
    if target:
        h, m, l = pieces(jnp.where(row == 3, 1.0, jnp.where(row == 4, norm, -2.0 * scaled)))
        out.append(jnp.concatenate([h, m, h, l, h, m], axis=0))
    return out


def twice(value):
    return jnp.concatenate([value, value], axis=1)


def left_half(shape):
    return lax.broadcasted_iota(jnp.int32, shape, 1) < 64


def store_source(slot, leaf, partner, center, fs, ms):
    (source,) = features(leaf[8:16], center, True, False)
    source = source.astype(BF16)
    lane = lax.broadcasted_iota(jnp.int32, partner.shape, 1).astype(F32)
    other = jnp.where(lane < leaf[11:12], partner, 0.0)
    moments = stacked(jnp.concatenate([leaf[0:8], other], axis=0))
    for b in range(4):
        fs[slot * 4 + b] = source[:, b * 128 : (b + 1) * 128]
        ms[slot * 4 + b] = moments[:, b * 128 : (b + 1) * 128]


def store_target(slot, leaf, center, ft):
    (target,) = features(leaf[8:16], center, False, True)
    target = target.astype(BF16)
    for b in range(2):
        ft[slot * 2 + b] = target[:, b * 256 : (b + 1) * 256]


def build_items(place, target_count, targets, empty, blocks, items):
    def per_leaf(i, n):
        nb = jnp.int32(0)
        for e in range(8):
            ok, slot, count = place(i, e)
            for b in range(4):
                blocks[nb + b] = slot * 4 + b
            nb = nb + jnp.where(ok, (count + 127) >> 7, 0)
        blocks[nb] = empty
        pairs = (nb + 1) >> 1

        def put(q, carry):
            code = (blocks[2 * q] << 9) | blocks[2 * q + 1]
            items[n + q] = code | ((2 * i) << 18)
            items[n + pairs + q] = code | ((2 * i + 1) << 18)
            return carry

        lax.fori_loop(0, pairs, put, 0)
        return n + jnp.where(target_count(i) > 256, 2 * pairs, pairs)

    n = lax.fori_loop(0, targets, per_leaf, jnp.int32(0))
    for t in range(2 * UNITS):
        items[n + t] = (empty << 9) | empty
    return n


def run_items(items, n, fs, ft, ms, acc, slots):
    def distances(code, u):
        left = jnp.concatenate([fs[(code >> 9) & 511], fs[code & 511]], axis=1)
        u[...] = dot(left, ft[code >> 18], CN)

    def contract(code, u):
        high, low = split(slope_of(u[...]))
        m = jnp.concatenate([ms[(code >> 9) & 511], ms[code & 511]], axis=1)
        acc[code >> 18] += dot(m, high, NN) + dot(m, low, NN)

    for s in range(UNITS):
        distances(items[s], slots[s])

    def body(t, carry):
        for s in range(UNITS):
            contract(items[UNITS * t + s], slots[s])
            distances(items[UNITS * (t + 1) + s], slots[s])
        return carry

    lax.fori_loop(0, (n + UNITS - 1) // UNITS, body, 0)


def moments_kernel(payload, leafp, own, center, pay2, dev, fp, *, leaves, factor):
    c = center[:, 0:1]
    (own_target,) = features(own[...], c, False, True)
    own_target = own_target.astype(BF16)[:, :64]

    def body(t, carry):
        for s in range(8):
            i = t * 8 + s
            leaf = payload[i]
            (target,) = features(leaf[8:16], c, False, True)
            (source,) = features(leafp[i], c, True, False)
            fp[i] = source
            basis = value_of(dot(target.astype(BF16), source.astype(BF16)[:, :64], CN))
            pay2[i, 0:8, :] = twice(exact_dot(leaf[0:8], basis, NN) * factor)
            pay2[i, 8:16, :] = leafp[i]
        return carry

    lax.fori_loop(0, leaves // 8, body, 0)
    half = left_half((FEATURES, 128))
    half8 = left_half((8, 128))
    total = jnp.zeros((8, 64), F32)
    for g in range(leaves // 8):
        sources, moments = [], []
        for q in range(4):
            i = 8 * g + 2 * q
            sources.append(jnp.where(half, fp[i], fp[i + 1]).astype(BF16))
            moments.append(jnp.where(half8, pay2[i, 0:8, :], pay2[i + 1, 0:8, :]))
        panel = value_of(dot(jnp.concatenate(sources, axis=1), own_target, CN))
        total = total + exact_dot(jnp.concatenate(moments, axis=1), panel, NN)
    dev[...] = twice(total * (1.0 / 64))


def assign(count_of, leaves, order):
    def tally(i, n):
        return n + (count_of(i) > 256).astype(jnp.int32)

    odd = lax.fori_loop(0, leaves, tally, jnp.int32(0)) & 1

    def deal(i, carry):
        large, taken = carry
        wide_leaf = (count_of(i) > 256).astype(jnp.int32)
        rank = jnp.where(wide_leaf == 1, large, i - large + odd)
        side = rank & 1
        place = jnp.where(side == 1, taken, i - taken)
        order[side * (leaves // 2) + place] = i
        return large + wide_leaf, taken + side

    lax.fori_loop(0, leaves, deal, (jnp.int32(0), jnp.int32(0)))


def clear_empty(empty, fs, ms):
    fs[empty] = jnp.zeros(fs.shape[1:], BF16)
    ms[empty] = jnp.zeros(ms.shape[1:], BF16)


def own_kernel(
    near, counts, me, payload, partner, center, acc,
    fs, ms, ft, blocks, items, order, *slots, leaves, targets,
):
    c = center[:, 0:1]
    assign(lambda i: counts[i], leaves, order)
    first = me[1] * targets

    def prep(t, carry):
        for s in range(2):
            i = 2 * t + s
            store_source(i, payload[i], partner[i], c, fs, ms)
        store_target(t, payload[order[first + t]], c, ft)
        return carry

    lax.fori_loop(0, leaves // 2, prep, 0)
    clear_empty(leaves * 4, fs, ms)
    acc[...] = jnp.zeros_like(acc)

    def place(i, e):
        j = near[order[first + i], e] - me[0] * leaves
        ok = (j >= 0) & (j < leaves)
        slot = jnp.where(ok, j, 0)
        return ok, slot, counts[slot]

    n = build_items(place, lambda i: counts[order[first + i]], targets, leaves * 4, blocks, items)
    run_items(items, n, fs, ft, ms, acc, slots)


def halo_kernel(
    near, counts, me, own, low, high, partner_low, partner_high, center, acc0,
    mine, theirs,
    acc, fs, ms, ft, blocks, items, order, *slots, leaves, targets, factor,
):
    c = center[:, 0:1]
    assign(lambda i: counts[leaves + i], leaves, order)
    first = me[1] * targets

    def prep(i, carry):
        store_source(i, low[i], partner_low[i], c, fs, ms)
        store_source(leaves + i, high[i], partner_high[i], c, fs, ms)
        return carry

    def prep_target(i, carry):
        store_target(i, own[order[first + i]], c, ft)
        return carry

    lax.fori_loop(0, leaves, prep, 0)
    lax.fori_loop(0, targets, prep_target, 0)
    empty = 2 * leaves * 4
    clear_empty(empty, fs, ms)
    acc[...] = acc0[...]

    def place(i, e):
        j = near[order[first + i], e] - (me[0] - 1) * leaves
        ok = (j < leaves) | (j >= 2 * leaves)
        slot = jnp.where(ok, jnp.where(j < leaves, j, j - leaves), 0)
        return ok, slot, counts[jnp.where(ok, j, 0)]

    n = build_items(place, lambda i: counts[leaves + order[first + i]], targets, empty, blocks, items)
    run_items(items, n, fs, ft, ms, acc, slots)
    scale = SLOPE * factor

    def finish(i, carry):
        for b in range(2):
            total = acc[2 * i + b]
            total = (total[0:16] + total[16:32]) * scale
            mine[i, :, b * 256 : (b + 1) * 256] = total[0:8]
            theirs[i, :, b * 256 : (b + 1) * 256] = total[8:16]
        return carry

    lax.fori_loop(0, targets, finish, 0)


def far_sum(lists, count, source_of, moment_of, target, across):
    half = left_half((FEATURES, 128))
    half8 = left_half((8, 128))
    total = jnp.zeros((8, 64), F32)
    for chunk in range(count // 8):
        sources, moments = [], []
        for q in range(4):
            a, b = lists(chunk * 8 + 2 * q), lists(chunk * 8 + 2 * q + 1)
            sources.append(jnp.where(half, source_of(a), source_of(b)).astype(BF16))
            moments.append(jnp.where(half8, moment_of(a), moment_of(b)))
        sources = jnp.concatenate(sources, axis=1)
        moments = jnp.concatenate(moments, axis=1)
        if across:
            columns = small_dot(moments, slope_of(dot(target, sources, CN)))
            total = columns if chunk == 0 else total + columns
        else:
            total = total + exact_dot(moments, slope_of(dot(sources, target, CN)), NN)
    return (joined(total) if across else total) * (SLOPE / 64)


class Strided:
    def __init__(self, array):
        self.array = array

    def __getitem__(self, n):
        return self.array[n * COPIES]


def upper_levels(coarse, me, box8, roots, c, fbs, fbt, pm, qm):
    def prep(t, carry):
        for s in range(8):
            b = 8 * t + s
            fbs[b], fbt[b] = features(box8[b], c, True, True)
        return carry

    lax.fori_loop(0, 7, prep, 0)
    half = left_half((FEATURES, 128))
    half8 = left_half((8, 128))

    def merge(child, parent, moments, out, count):
        def body(t, carry):
            for s in range(8):
                m = t * 8 + s
                source = jnp.where(half, fbs[child + 2 * m], fbs[child + 2 * m + 1]).astype(BF16)
                target = fbt[parent + m].astype(BF16)[:, :64]
                panel = value_of(dot(source, target, CN))
                pair = jnp.where(half8, moments[2 * m], moments[2 * m + 1])
                out[m] = twice(exact_dot(pair, panel, NN) * (1.0 / 64))
            return carry

        lax.fori_loop(0, count // 8, body, 0)

    merge(0, 32, Strided(roots), pm, 16)
    merge(32, 48, pm, qm, 8)
    n = me
    m = n >> 1
    t = n >> 2

    def far(base, row, moments):
        target = fbt[row].astype(BF16)[:, :64]
        return far_sum(
            lambda e: coarse[row, e], 16, lambda b: fbs[base + b], lambda b: moments[b], target, False
        )

    def down(local, source, target):
        panel = value_of(dot(fbs[source].astype(BF16)[:, :64], fbt[target].astype(BF16)[:, :64], CN))
        return exact_dot(local, panel, NN) * (1.0 / 64)

    quad = far(48, 48 + t, qm)
    pair = down(quad, 48 + t, 32 + m) + far(32, 32 + m, pm)
    return down(pair, 32 + m, n) + far(0, n, Strided(roots))


def far_kernel(
    far, coarse, counts, me, own, pay_own, pay_low, pay_high, box8, roots, center,
    out,
    fps, fpt, mps, fbs, fbt, pm, qm, local,
    *, leaves, factor,
):
    c = center[:, 0:1]

    def prep_far(t, carry):
        for s in range(4):
            i = t * 4 + s
            for k, page in enumerate((pay_low, pay_own, pay_high)):
                (fps[k * leaves + i],) = features(page[i, 8:16], c, True, False)
                mps[k * leaves + i] = page[i, 0:8]
            (fpt[i],) = features(pay_own[i, 8:16], c, False, True)
        return carry

    lax.fori_loop(0, leaves // 4, prep_far, 0)
    dev = me[0]
    base = (dev - 1) * leaves

    def gather(t, carry):
        for s in range(4):
            i = t * 4 + s
            target = fpt[i].astype(BF16)[:, :64]
            local[i] = far_sum(
                lambda e: far[i, e] - base, 32, lambda b: fps[b], lambda b: mps[b], target, ACROSS
            )
        return carry

    lax.fori_loop(0, leaves // 4, gather, 0)
    local_dev = upper_levels(coarse, dev, box8, roots, c, fbs, fbt, pm, qm)
    own_source = fbs[dev].astype(BF16)[:, :64]

    def down(t, carry):
        for s in range(8):
            i = t * 8 + s
            target = fpt[i].astype(BF16)[:, :64]
            panel = value_of(dot(own_source, target, CN))
            local[i] += exact_dot(local_dev, panel, NN) * (1.0 / 64)
        return carry

    lax.fori_loop(0, leaves // 8, down, 0)

    def finish(t, carry):
        for s in range(8):
            i = t * 8 + s
            source = fps[leaves + i].astype(BF16)[:, :64]
            (points,) = features(own[i, 8:16], c, False, True)
            basis = value_of(dot(source, points.astype(BF16), CN))
            out[i] = exact_dot(local[i], basis, NN) * factor
        return carry

    lax.fori_loop(0, leaves // 8, finish, 0)


def sum_kernel(counts, me, far, mine, back, out, order, *, leaves):
    assign(lambda i: counts[i], leaves, order)
    half = leaves // 2
    lane = lax.broadcasted_iota(jnp.int32, far.shape[1:], 1)

    def body(t, carry):
        for s in range(4):
            k = 4 * t + s
            for side, part in ((me[1], mine), (1 - me[1], back)):
                i = order[side * half + k]
                out[i] = jnp.where(lane < counts[i], far[i] + part[k], 0.0)
        return carry

    lax.fori_loop(0, half // 4, body, 0)


def cost(microseconds):
    flops = int(microseconds * 1.1e9)
    return pl.CostEstimate(flops=flops, transcendentals=0, bytes_accessed=1 << 20)


def wide(array):
    rows = jnp.concatenate([array, array], axis=2)
    return jnp.pad(rows, ((0, 0), (0, 8 - array.shape[1]), (0, 0)))


def local(points, probes, counts, near_list, far_list, coarse_list, leaf_proxy, box_proxy):
    leaves = points.shape[0]
    size = points.shape[2]
    nodes = lax.axis_size("space")
    device = lax.axis_index("space")
    factor = size ** (-0.5)
    slot = lax.broadcasted_iota(jnp.int32, (leaves, 1, size), 2)
    masked = jnp.where(slot < counts[:, None, None], probes, 0.0)
    count_row = jnp.broadcast_to(counts.astype(F32)[:, None, None], (leaves, 5, size))
    payload = jnp.concatenate([masked, points, count_row], axis=1)
    forward = [(i, i + 1) for i in range(nodes - 1)]
    backward = [(i + 1, i) for i in range(nodes - 1)]
    pairs = [(i, i ^ 1) for i in range(lax.axis_size("probe"))]
    partner = lax.ppermute(probes, "probe", pairs)
    low = lax.ppermute(payload, "space", forward)
    high = lax.ppermute(payload, "space", backward)
    partner_low = lax.ppermute(partner, "space", forward)
    partner_high = lax.ppermute(partner, "space", backward)
    leafp = wide(leaf_proxy)
    box8 = wide(box_proxy)
    center = jnp.broadcast_to(jnp.pad(points[0, :, 0], (0, 5))[:, None], (8, 128))
    own = lax.dynamic_index_in_dim(box8, device, 0, keepdims=False)
    half = lax.axis_index("probe") & 1
    me = jnp.stack([device, half]).astype(jnp.int32)
    params = pltpu.CompilerParams(vmem_limit_bytes=56 << 20)
    vm = pltpu.VMEM
    vmem = pl.BlockSpec(memory_space=vm)
    smem = pl.BlockSpec(memory_space=pltpu.SMEM)
    shape = jax.ShapeDtypeStruct
    pay2, dev = pl.pallas_call(
        functools.partial(moments_kernel, leaves=leaves, factor=factor),
        out_shape=(shape((leaves, 16, 128), F32), shape((8, 128), F32)),
        in_specs=[vmem] * 4,
        out_specs=(vmem, vmem),
        scratch_shapes=[vm((leaves, FEATURES, 128), F32)],
        compiler_params=params,
        cost_estimate=cost(8),
        name="moments",
    )(payload, leafp, own, center)
    low2 = lax.ppermute(pay2, "space", forward)
    high2 = lax.ppermute(pay2, "space", backward)
    copies = jnp.broadcast_to(dev[None], (COPIES, 8, 128))
    roots = lax.all_gather(copies, "space", axis=0, tiled=True)
    targets = leaves // 2

    def work(blocks):
        return (
            [
                vm((blocks, FEATURES, 128), BF16),
                vm((blocks, 32, 128), BF16),
                vm((targets * 2, FEATURES, 256), BF16),
                pltpu.SMEM((48,), jnp.int32),
                pltpu.SMEM((targets * 32 + 64,), jnp.int32),
                pltpu.SMEM((leaves,), jnp.int32),
            ]
            + [vm((256, 256), F32)] * UNITS
        )

    acc0 = pl.pallas_call(
        functools.partial(own_kernel, leaves=leaves, targets=targets),
        out_shape=shape((targets * 2, 32, 256), F32),
        in_specs=[smem] * 3 + [vmem] * 3,
        out_specs=vmem,
        scratch_shapes=work(leaves * 4 + 1),
        compiler_params=params,
        cost_estimate=cost(28),
        name="near_own",
    )(near_list, counts, me, payload, partner, center)
    low, high, low2, high2 = lax.optimization_barrier((low, high, low2, high2))
    counts3 = jnp.concatenate(
        [low[:, 11, 0].astype(jnp.int32), counts, high[:, 11, 0].astype(jnp.int32)]
    )
    mine, theirs = pl.pallas_call(
        functools.partial(halo_kernel, leaves=leaves, targets=targets, factor=factor),
        out_shape=(shape((targets, 8, size), F32),) * 2,
        in_specs=[smem] * 3 + [vmem] * 7,
        out_specs=(vmem, vmem),
        scratch_shapes=[vm((targets * 2, 32, 256), F32)] + work(2 * leaves * 4 + 1),
        compiler_params=params,
        cost_estimate=cost(30),
        name="near_halo",
    )(near_list, counts3, me, payload, low, high, partner_low, partner_high, center, acc0)
    back = lax.ppermute(theirs, "probe", pairs)
    far = pl.pallas_call(
        functools.partial(far_kernel, leaves=leaves, factor=factor),
        out_shape=shape(probes.shape, F32),
        in_specs=[smem] * 4 + [vmem] * 7,
        out_specs=vmem,
        scratch_shapes=[
            vm((3 * leaves, FEATURES, 128), F32),
            vm((leaves, FEATURES, 128), F32),
            vm((3 * leaves, 8, 128), F32),
            vm((56, FEATURES, 128), F32),
            vm((56, FEATURES, 128), F32),
            vm((nodes // 2, 8, 128), F32),
            vm((nodes // 4, 8, 128), F32),
            vm((leaves, 8, 64), F32),
        ],
        compiler_params=params,
        cost_estimate=cost(30),
        name="far",
    )(far_list, coarse_list, counts, me, payload, pay2, low2, high2, box8, roots, center)
    return pl.pallas_call(
        functools.partial(sum_kernel, leaves=leaves),
        out_shape=shape(probes.shape, F32),
        in_specs=[smem] * 2 + [vmem] * 3,
        out_specs=vmem,
        scratch_shapes=[pltpu.SMEM((leaves,), jnp.int32)],
        compiler_params=params,
        name="sum",
    )(counts, me, far, mine, back)


def solution(mesh):
    return jax.shard_map(
        local,
        mesh=mesh,
        in_specs=(
            P("space", None, None),
            P("space", "probe", None),
            P("space"),
            P("space", None),
            P("space", None),
            P(),
            P("space", None, None),
            P(),
        ),
        out_specs=P("space", "probe", None),
        check_vma=False,
    )
```

profile of v0, /device:TPU:8, one launch (start us, length us, event | category | flops | bytes accessed | tf_op | source)
XLA Modules:
  0.0 152.5 jit_solution(2281322695407007793)
XLA Ops:
  6.5 0.0 copy-start.6
  6.5 0.0 all-gather.2.cloned.1.call-start
  6.5 1.9 %collective-permute-start.4 = (f32[32,8,512]{2,1,0:T(8,128)}, f32[32,8,512]{2,1,0:T(8,128)}, u32[]{:S(2)}, u32[]{:S(2)}) collective-permute-start(f32[32,8,512]{2,1,0:T(8,128)} %param.9), channel_id=1, source_target_pairs={{0,1},{1,0},{2,3},{3,2},{4,5},{5,4},{6,7},{7,6},{8,9},{9,8},{10,11... | collective-permute-start | bytes 1572872 | tf_op jit(solution)/shard_map/ppermute | solution.py:462
  8.5 0.0 copy-done.6
  8.5 0.1 iota_compare_fusion.2
  8.5 1.1 copy.25
  9.6 0.8 slice_reduce_fusion
  10.4 0.0 copy-start.4
  10.4 1.1 broadcast_select_fusion
  11.6 0.0 copy-done.4
  11.6 0.0 copy-start.3
  11.6 0.8 select_maximum_fusion.1.leafp
  12.4 0.1 copy-done.3
  12.5 0.1 select_maximum_fusion.box8
  12.7 0.0 copy-start.2
  12.7 0.7 dynamic-slice_bitcast_fusion.own
  13.4 0.1 broadcast_in_dim.20
  13.5 0.0 copy-done.2
  13.5 1.1 pad_maximum_fusion.payload.own
  14.6 0.7 broadcast_in_dim.34.center
  15.3 0.0 copy-start
  15.3 0.0 copy-start.5
  15.3 8.4 %moments.1 = (f32[32,16,128]{2,1,0:T(8,128)}, f32[8,128]{1,0:T(8,128)}) custom-call(f32[32,16,512]{2,1,0:T(8,128)} %pad_maximum_fusion.payload.own, f32[32,8,128]{2,1,0:T(8,128)} %select_maximum_fusion.1.leafp, f32[8,128]{1,0:T(8,128)} %dynamic-slice_bitcast_fusion.own, f32[8,128]{1,0:T(8,128)} %broadcast_in_dim.34.center), custom_call_target="tpu_custom_call" | custom-call | flops 8800000000 | bytes 1048576 | tf_op jit(solution)/shard_map/moments/pallas_call | solution.py:478
  23.7 1.9 %collective-permute-start.2 = (f32[32,16,128]{2,1,0:T(8,128)}, f32[32,16,128]{2,1,0:T(8,128)S(1)}, u32[]{:S(2)}, u32[]{:S(2)}) collective-permute-start(f32[32,16,128]{2,1,0:T(8,128)} %get-tuple-element.13.pay_own), channel_id=1, source_target_pairs={{0,4},{4,8},{8,12},{12,16},{16,20},{20,24},{24,28},{28,32},{32,36}... | collective-permute-start | bytes 786440 | tf_op jit(solution)/shard_map/ppermute | solution.py:488
  25.6 0.0 copy-done
  25.6 3.5 %collective-permute-start = (f32[32,16,512]{2,1,0:T(8,128)S(1)}, f32[32,16,512]{2,1,0:T(8,128)S(1)}, u32[]{:S(2)}, u32[]{:S(2)}) collective-permute-start(f32[32,16,512]{2,1,0:T(8,128)S(1)} %copy-done), channel_id=1, source_target_pairs={{0,4},{4,8},{8,12},{12,16},{16,20},{20,24},{24,28},{28,32},{32,36}... | collective-permute-start | bytes 3145736 | tf_op jit(solution)/shard_map/ppermute | solution.py:463
  29.1 4.2 %collective-permute-start.1 = (f32[32,16,512]{2,1,0:T(8,128)S(1)}, f32[32,16,512]{2,1,0:T(8,128)S(1)}, u32[]{:S(2)}, u32[]{:S(2)}) collective-permute-start(f32[32,16,512]{2,1,0:T(8,128)S(1)} %copy-done), channel_id=1, source_target_pairs={{4,0},{8,4},{12,8},{16,12},{20,16},{24,20},{28,24},{32,28},{36,32}... | collective-permute-start | bytes 3145736 | tf_op jit(solution)/shard_map/ppermute | solution.py:464
  33.3 2.4 %collective-permute-start.3 = (f32[32,16,128]{2,1,0:T(8,128)}, f32[32,16,128]{2,1,0:T(8,128)}, u32[]{:S(2)}, u32[]{:S(2)}) collective-permute-start(f32[32,16,128]{2,1,0:T(8,128)} %get-tuple-element.13.pay_own), channel_id=1, source_target_pairs={{4,0},{8,4},{12,8},{16,12},{20,16},{24,20},{28,24},{32,28},{36,32}... | collective-permute-start | bytes 786440 | tf_op jit(solution)/shard_map/ppermute | solution.py:489
  35.7 1.3 broadcast_in_dim.35
  37.0 0.0 all-gather.2.cloned.1.call-update
  37.0 0.0 copy-done.5
  37.0 0.0 copy-start.8
  37.0 0.7 copy.30.coarse
  37.7 0.0 copy-done.8
  37.7 0.7 copy.32.near
  38.4 0.7 pad_add_fusion.me
  39.1 0.0 collective-permute-done.4.partner
  39.1 1.9 %collective-permute-start.5 = (f32[32,8,512]{2,1,0:T(8,128)}, f32[32,8,512]{2,1,0:T(8,128)S(1)}, u32[]{:S(2)}, u32[]{:S(2)}) collective-permute-start(f32[32,8,512]{2,1,0:T(8,128)} %collective-permute-done.4.partner), channel_id=1, source_target_pairs={{0,4},{4,8},{8,12},{12,16},{16,20},{20,24},{24,28},{28,32},{32,36}... | collective-permute-start | bytes 1572872 | tf_op jit(solution)/shard_map/ppermute | solution.py:465
  41.0 0.0 collective-permute-done.2.pay_low
  41.0 0.0 copy-start.13
  41.0 5.8 %collective-permute-start.6 = (f32[32,8,512]{2,1,0:T(8,128)}, f32[32,8,512]{2,1,0:T(8,128)S(1)}, u32[]{:S(2)}, u32[]{:S(2)}) collective-permute-start(f32[32,8,512]{2,1,0:T(8,128)} %collective-permute-done.4.partner), channel_id=1, source_target_pairs={{4,0},{8,4},{12,8},{16,12},{20,16},{24,20},{28,24},{32,28},{36,32}... | collective-permute-start | bytes 1572872 | tf_op jit(solution)/shard_map/ppermute | solution.py:466
  46.8 23.9 %near_own.1.acc0 = f32[32,32,256]{2,1,0:T(8,128)} custom-call(s32[32,8]{1,0:T(8,128)} %copy.32.near, s32[32]{0:T(128)} %counts.5, s32[2]{0:T(128)} %pad_add_fusion.me, f32[32,16,512]{2,1,0:T(8,128)} %pad_maximum_fusion.payload.own, f32[32,8,512]{2,1,0:T(8,128)} %collective-permute-done.4.partner, f32[8,128]{1,0:T(8,128)} %broadcast_in_dim.34.center), custom_call_target="tpu_custom_call" | custom-call | flops 30799998976 | bytes 1048576 | tf_op jit(solution)/shard_map/near_own/pallas_call | solution.py:507
  70.7 0.0 copy-done.13
  70.7 0.0 collective-permute-done.3.pay_high
  70.7 0.0 collective-permute-done.low
  70.7 0.0 copy-start.9
  70.7 0.0 collective-permute-done.1.high
  70.7 0.0 copy-start.10
  70.7 1.2 convert_reduce_fusion
  72.0 0.0 copy-start.7
  72.0 0.7 copy-done.7
  72.6 0.6 pad_add_fusion.1.counts
  73.2 0.0 collective-permute-done.5.partner_low
  73.3 0.0 collective-permute-done.6.partner_high
  73.3 0.0 copy-done.9
  73.3 0.0 copy-done.10
  73.3 0.8 copy-done.11
  74.0 0.8 copy-done.12
  74.9 30.7 %near_halo.1 = (f32[16,8,512]{2,1,0:T(8,128)}, f32[16,8,512]{2,1,0:T(8,128)}) custom-call(s32[32,8]{1,0:T(8,128)} %copy.32.near, s32[96]{0:T(128)} %pad_add_fusion.1.counts, s32[2]{0:T(128)} %pad_add_fusion.me, f32[32,16,512]{2,1,0:T(8,128)} %pad_maximum_fusion.payload.own, f32[32,16,512]{2,1,0:T(8,128)} %copy-done.9, f32[32,16,512]{2,1,0:T(8,128)} %copy-done.10, ...), custom_call_target="tpu_custom_call" | custom-call | flops 32999999488 | bytes 1048576 | tf_op jit(solution)/shard_map/near_halo/pallas_call | solution.py:521
  105.5 2.5 %collective-permute-start.7 = (f32[16,8,512]{2,1,0:T(8,128)}, f32[16,8,512]{2,1,0:T(8,128)S(1)}, u32[]{:S(2)}, u32[]{:S(2)}) collective-permute-start(f32[16,8,512]{2,1,0:T(8,128)} %get-tuple-element.20), channel_id=1, source_target_pairs={{0,1},{1,0},{2,3},{3,2},{4,5},{5,4},{6,7},{7,6},{8,9},{9,8},{10,11... | collective-permute-start | bytes 786440 | tf_op jit(solution)/shard_map/ppermute | solution.py:531
  108.1 34.1 %far.2 = f32[32,8,512]{2,1,0:T(8,128)} custom-call(s32[32,32]{1,0:T(8,128)} %far.3, s32[56,16]{1,0:T(8,128)} %copy.30.coarse, s32[32]{0:T(128)} %counts.5, s32[2]{0:T(128)} %pad_add_fusion.me, f32[32,16,512]{2,1,0:T(8,128)} %pad_maximum_fusion.payload.own, f32[32,16,128]{2,1,0:T(8,128)} %get-tuple-element.13.pay_own, f32[32,16,128]{2,1,0:T(8,128)} %copy-done.13, ...), custom_call_target="tpu_custom_call" | custom-call | flops 32999999488 | bytes 1048576 | tf_op jit(solution)/shard_map/far/pallas_call | solution.py:532
  142.2 0.0 collective-permute-done.7.back
  142.2 0.7 copy-done.1
  142.8 2.8 %sum.1 = f32[32,8,512]{2,1,0:T(8,128)} custom-call(s32[32]{0:T(128)} %counts.5, s32[2]{0:T(128)} %pad_add_fusion.me, f32[32,8,512]{2,1,0:T(8,128)} %far.2, f32[16,8,512]{2,1,0:T(8,128)} %get-tuple-element.19.mine, f32[16,8,512]{2,1,0:T(8,128)} %copy-done.1), custom_call_target="tpu_custom_call" | custom-call | tf_op jit(solution)/shard_map/sum/pallas_call | solution.py:551
  (8 shorter events, 0.1 us)
Async XLA Ops:
  6.5 1.9 %copy-start.6 = (s32[32]{0:T(128)S(1)}, s32[32]{0:T(128)}, u32[]{:S(2)}) copy-start(s32[32]{0:T(128)} %counts.5) | copy-start | bytes 388
  6.5 101.5 %all-gather.2.cloned.1.call-start = ((), (), s32[]{:S(2)}) async-start(), calls=%async_computation | async-start | bytes 1081344 | tf_op jit(solution)/shard_map/all_gather | solution.py:491
  6.5 32.5 %collective-permute-start.4 = (f32[32,8,512]{2,1,0:T(8,128)}, f32[32,8,512]{2,1,0:T(8,128)}, u32[]{:S(2)}, u32[]{:S(2)}) collective-permute-start(f32[32,8,512]{2,1,0:T(8,128)} %param.9), channel_id=1, source_target_pairs={{0,1},{1,0},{2,3},{3,2},{4,5},{5,4},{6,7},{7,6},{8,9},{9,8},{10,11... | collective-permute-start | bytes 1572872 | tf_op jit(solution)/shard_map/ppermute | solution.py:462
  10.4 1.1 copy-start.4
  11.6 0.9 copy-start.3
  12.7 0.8 copy-start.2
  15.3 10.3 %copy-start = (f32[32,16,512]{2,1,0:T(8,128)S(1)}, f32[32,16,512]{2,1,0:T(8,128)}, u32[]{:S(2)}) copy-start(f32[32,16,512]{2,1,0:T(8,128)} %pad_maximum_fusion.payload.own) | copy-start | bytes 3145732
  15.3 21.8 %copy-start.5 = (s32[56,16]{0,1:T(8,128)S(1)}, s32[56,16]{0,1:T(8,128)}, u32[]{:S(2)}) copy-start(s32[56,16]{0,1:T(8,128)} %param.13) | copy-start | bytes 10756
  23.7 17.3 %collective-permute-start.2 = (f32[32,16,128]{2,1,0:T(8,128)}, f32[32,16,128]{2,1,0:T(8,128)S(1)}, u32[]{:S(2)}, u32[]{:S(2)}) collective-permute-start(f32[32,16,128]{2,1,0:T(8,128)} %get-tuple-element.13.pay_own), channel_id=1, source_target_pairs={{0,4},{4,8},{8,12},{12,16},{16,20},{20,24},{24,28},{28,32},{32,36}... | collective-permute-start | bytes 786440 | tf_op jit(solution)/shard_map/ppermute | solution.py:488
  25.6 45.1 %collective-permute-start = (f32[32,16,512]{2,1,0:T(8,128)S(1)}, f32[32,16,512]{2,1,0:T(8,128)S(1)}, u32[]{:S(2)}, u32[]{:S(2)}) collective-permute-start(f32[32,16,512]{2,1,0:T(8,128)S(1)} %copy-done), channel_id=1, source_target_pairs={{0,4},{4,8},{8,12},{12,16},{16,20},{20,24},{24,28},{28,32},{32,36}... | collective-permute-start | bytes 3145736 | tf_op jit(solution)/shard_map/ppermute | solution.py:463
  29.1 41.6 %collective-permute-start.1 = (f32[32,16,512]{2,1,0:T(8,128)S(1)}, f32[32,16,512]{2,1,0:T(8,128)S(1)}, u32[]{:S(2)}, u32[]{:S(2)}) collective-permute-start(f32[32,16,512]{2,1,0:T(8,128)S(1)} %copy-done), channel_id=1, source_target_pairs={{4,0},{8,4},{12,8},{16,12},{20,16},{24,20},{28,24},{32,28},{36,32}... | collective-permute-start | bytes 3145736 | tf_op jit(solution)/shard_map/ppermute | solution.py:464
  33.3 37.4 %collective-permute-start.3 = (f32[32,16,128]{2,1,0:T(8,128)}, f32[32,16,128]{2,1,0:T(8,128)}, u32[]{:S(2)}, u32[]{:S(2)}) collective-permute-start(f32[32,16,128]{2,1,0:T(8,128)} %get-tuple-element.13.pay_own), channel_id=1, source_target_pairs={{4,0},{8,4},{12,8},{16,12},{20,16},{24,20},{28,24},{32,28},{36,32}... | collective-permute-start | bytes 786440 | tf_op jit(solution)/shard_map/ppermute | solution.py:489
  37.0 0.7 copy-start.8
  39.1 34.2 %collective-permute-start.5 = (f32[32,8,512]{2,1,0:T(8,128)}, f32[32,8,512]{2,1,0:T(8,128)S(1)}, u32[]{:S(2)}, u32[]{:S(2)}) collective-permute-start(f32[32,8,512]{2,1,0:T(8,128)} %collective-permute-done.4.partner), channel_id=1, source_target_pairs={{0,4},{4,8},{8,12},{12,16},{16,20},{20,24},{24,28},{28,32},{32,36}... | collective-permute-start | bytes 1572872 | tf_op jit(solution)/shard_map/ppermute | solution.py:465
  41.0 29.7 %copy-start.13 = (f32[32,16,128]{2,1,0:T(8,128)}, f32[32,16,128]{2,1,0:T(8,128)S(1)}, u32[]{:S(2)}) copy-start(f32[32,16,128]{2,1,0:T(8,128)S(1)} %collective-permute-done.2.pay_low) | copy-start | bytes 786436
  41.0 32.3 %collective-permute-start.6 = (f32[32,8,512]{2,1,0:T(8,128)}, f32[32,8,512]{2,1,0:T(8,128)S(1)}, u32[]{:S(2)}, u32[]{:S(2)}) collective-permute-start(f32[32,8,512]{2,1,0:T(8,128)} %collective-permute-done.4.partner), channel_id=1, source_target_pairs={{4,0},{8,4},{12,8},{16,12},{20,16},{24,20},{28,24},{32,28},{36,32}... | collective-permute-start | bytes 1572872 | tf_op jit(solution)/shard_map/ppermute | solution.py:466
  70.7 2.6 %copy-start.9 = (f32[32,16,512]{2,1,0:T(8,128)}, f32[32,16,512]{2,1,0:T(8,128)S(1)}, u32[]{:S(2)}) copy-start(f32[32,16,512]{2,1,0:T(8,128)S(1)} %collective-permute-done.low) | copy-start | bytes 3145732
  70.7 2.6 %copy-start.10 = (f32[32,16,512]{2,1,0:T(8,128)}, f32[32,16,512]{2,1,0:T(8,128)S(1)}, u32[]{:S(2)}) copy-start(f32[32,16,512]{2,1,0:T(8,128)S(1)} %collective-permute-done.1.high) | copy-start | bytes 3145732
  72.0 0.7 copy-start.7
  73.3 0.8 copy-start.11
  74.0 0.8 copy-start.12
  105.5 36.6 %collective-permute-start.7 = (f32[16,8,512]{2,1,0:T(8,128)}, f32[16,8,512]{2,1,0:T(8,128)S(1)}, u32[]{:S(2)}, u32[]{:S(2)}) collective-permute-start(f32[16,8,512]{2,1,0:T(8,128)} %get-tuple-element.20), channel_id=1, source_target_pairs={{0,1},{1,0},{2,3},{3,2},{4,5},{5,4},{6,7},{7,6},{8,9},{9,8},{10,11... | collective-permute-start | bytes 786440 | tf_op jit(solution)/shard_map/ppermute | solution.py:531
  142.2 0.7 copy-start.1
Sparse Core Ops, SparseCore 0:
  37.1 42.6 all-gather.1
where the time goes:
time: 155 us; the launch traced here: 152 us
  Pallas kernels  99.9 us (64%)
  starting transfers between devices  24.1 us (16%)
  between operations  13.6 us (9%)
  local copies, waits for them, and re-layouts  9.1 us (6%)
  other arithmetic  5.74 us (4%)
    pallas_call x1, Pallas kernels, local(): pl.pallas_call(functools.partial(far_kernel, leaves=leaves, factor=factor...  34.1 us
    pallas_call x1, Pallas kernels, local(): pl.pallas_call(functools.partial(halo_kernel, leaves=leaves, targets=targ...  30.7 us
    pallas_call x1, Pallas kernels, local(): pl.pallas_call(functools.partial(own_kernel, leaves=leaves, targets=targe...  23.9 us
    pallas_call x1, Pallas kernels, local(): pl.pallas_call(functools.partial(moments_kernel, leaves=leaves, factor=fa...  8.42 us
    ppermute x1, starting transfers between devices, local(): partner_high = lax.ppermute(partner, 'space', backward)  5.75 us
    unnamed x33, local copies, waits for them, and re-layouts  5.59 us
    ppermute x1, starting transfers between devices, local(): high = lax.ppermute(payload, 'space', backward)  4.17 us
    ppermute x1, starting transfers between devices, local(): low = lax.ppermute(payload, 'space', forward)  3.5 us
  transfers between devices with their start and end apart: 9, of which 0 were waited for; matrix products, arithmetic and copies ran while one was open for 8% of the time, Pallas kernels for 64%

commit v1 on v0

--- a/solution.py
+++ b/solution.py
@@ -17,7 +17,6 @@
 FEATURES = 48
 UNITS = 8
 ACROSS = False
-COPIES = 8
 CN = (((0,), (0,)), ((), ()))
 NT = (((1,), (1,)), ((), ()))
 NN = (((1,), (0,)), ((), ()))
@@ -96,19 +95,28 @@
     return lax.broadcasted_iota(jnp.int32, shape, 1) < 64
 
 
-def store_source(slot, leaf, partner, center, fs, ms):
-    (source,) = features(leaf[8:16], center, True, False)
+def lanes_of(page, i, start):
+    return jnp.concatenate([page[i, 16 * b + start : 16 * b + start + 8, :] for b in range(4)], axis=1)
+
+
+def center_of(page):
+    return page[0, 8:16, 0:1]
+
+
+def store_source(slot, page, i, partner, center, fs, ms):
+    rows = lanes_of(page, i, 8)
+    (source,) = features(rows, center, True, False)
     source = source.astype(BF16)
     lane = lax.broadcasted_iota(jnp.int32, partner.shape, 1).astype(F32)
-    other = jnp.where(lane < leaf[11:12], partner, 0.0)
-    moments = stacked(jnp.concatenate([leaf[0:8], other], axis=0))
+    other = jnp.where(lane < rows[3:4], partner, 0.0)
+    moments = stacked(jnp.concatenate([lanes_of(page, i, 0), other], axis=0))
     for b in range(4):
         fs[slot * 4 + b] = source[:, b * 128 : (b + 1) * 128]
         ms[slot * 4 + b] = moments[:, b * 128 : (b + 1) * 128]
 
 
-def store_target(slot, leaf, center, ft):
-    (target,) = features(leaf[8:16], center, False, True)
+def store_target(slot, page, i, center, ft):
+    (target,) = features(lanes_of(page, i, 8), center, False, True)
     target = target.astype(BF16)
     for b in range(2):
         ft[slot * 2 + b] = target[:, b * 256 : (b + 1) * 256]
@@ -162,21 +170,36 @@
     lax.fori_loop(0, (n + UNITS - 1) // UNITS, body, 0)
 
 
-def moments_kernel(payload, leafp, own, center, pay2, dev, fp, *, leaves, factor):
-    c = center[:, 0:1]
-    (own_target,) = features(own[...], c, False, True)
-    own_target = own_target.astype(BF16)[:, :64]
+def rows_of(planes, i, extra):
+    rows = [planes[d, pl.ds(i, 1), :] for d in range(3)]
+    width = rows[0].shape[1]
+    return jnp.concatenate(
+        rows + [jnp.full((1, width), extra, F32), jnp.zeros((4, width), F32)], axis=0
+    )
+
+
+def moments_kernel(counts, me, probes, points, leafp, boxp, page, dev, fp, *, leaves, factor):
+    c = rows_of(points, 0, 0.0)[:, 0:1]
+    (own_target,) = features(rows_of(boxp, me[0], 0.0), c, False, True)
+    own_target = own_target.astype(BF16)
+    lane = lax.broadcasted_iota(jnp.int32, probes.shape[1:], 1)
 
     def body(t, carry):
         for s in range(8):
             i = t * 8 + s
-            leaf = payload[i]
-            (target,) = features(leaf[8:16], c, False, True)
-            (source,) = features(leafp[i], c, True, False)
+            count = counts[i]
+            masked = jnp.where(lane < count, probes[i], 0.0)
+            rows = rows_of(points, i, count.astype(F32))
+            for b in range(4):
+                page[i, 16 * b : 16 * b + 8, :] = masked[:, b * 128 : (b + 1) * 128]
+                page[i, 16 * b + 8 : 16 * b + 16, :] = rows[:, b * 128 : (b + 1) * 128]
+            proxies = twice(rows_of(leafp, i, 0.0))
+            (target,) = features(rows, c, False, True)
+            (source,) = features(proxies, c, True, False)
             fp[i] = source
             basis = value_of(dot(target.astype(BF16), source.astype(BF16)[:, :64], CN))
-            pay2[i, 0:8, :] = twice(exact_dot(leaf[0:8], basis, NN) * factor)
-            pay2[i, 8:16, :] = leafp[i]
+            page[i, 64:72, :] = twice(exact_dot(masked, basis, NN) * factor)
+            page[i, 72:80, :] = proxies
         return carry
 
     lax.fori_loop(0, leaves // 8, body, 0)
@@ -188,7 +211,7 @@
         for q in range(4):
             i = 8 * g + 2 * q
             sources.append(jnp.where(half, fp[i], fp[i + 1]).astype(BF16))
-            moments.append(jnp.where(half8, pay2[i, 0:8, :], pay2[i + 1, 0:8, :]))
+            moments.append(jnp.where(half8, page[i, 64:72, :], page[i + 1, 64:72, :]))
         panel = value_of(dot(jnp.concatenate(sources, axis=1), own_target, CN))
         total = total + exact_dot(jnp.concatenate(moments, axis=1), panel, NN)
     dev[...] = twice(total * (1.0 / 64))
@@ -218,18 +241,18 @@
 
 
 def own_kernel(
-    near, counts, me, payload, partner, center, acc,
+    near, counts, me, page, partner, acc,
     fs, ms, ft, blocks, items, order, *slots, leaves, targets,
 ):
-    c = center[:, 0:1]
+    c = center_of(page)
     assign(lambda i: counts[i], leaves, order)
     first = me[1] * targets
 
     def prep(t, carry):
         for s in range(2):
             i = 2 * t + s
-            store_source(i, payload[i], partner[i], c, fs, ms)
-        store_target(t, payload[order[first + t]], c, ft)
+            store_source(i, page, i, partner[i], c, fs, ms)
+        store_target(t, page, order[first + t], c, ft)
         return carry
 
     lax.fori_loop(0, leaves // 2, prep, 0)
@@ -237,7 +260,7 @@
     acc[...] = jnp.zeros_like(acc)
 
     def place(i, e):
-        j = near[order[first + i], e] - me[0] * leaves
+        j = near[e, order[first + i]] - me[0] * leaves
         ok = (j >= 0) & (j < leaves)
         slot = jnp.where(ok, j, 0)
         return ok, slot, counts[slot]
@@ -247,21 +270,21 @@
 
 
 def halo_kernel(
-    near, counts, me, own, low, high, partner_low, partner_high, center, acc0,
+    near, counts, me, own, low, high, partner_low, partner_high, acc0,
     mine, theirs,
     acc, fs, ms, ft, blocks, items, order, *slots, leaves, targets, factor,
 ):
-    c = center[:, 0:1]
+    c = center_of(own)
     assign(lambda i: counts[leaves + i], leaves, order)
     first = me[1] * targets
 
     def prep(i, carry):
-        store_source(i, low[i], partner_low[i], c, fs, ms)
-        store_source(leaves + i, high[i], partner_high[i], c, fs, ms)
+        store_source(i, low, i, partner_low[i], c, fs, ms)
+        store_source(leaves + i, high, i, partner_high[i], c, fs, ms)
         return carry
 
     def prep_target(i, carry):
-        store_target(i, own[order[first + i]], c, ft)
+        store_target(i, own, order[first + i], c, ft)
         return carry
 
     lax.fori_loop(0, leaves, prep, 0)
@@ -271,7 +294,7 @@
     acc[...] = acc0[...]
 
     def place(i, e):
-        j = near[order[first + i], e] - (me[0] - 1) * leaves
+        j = near[e, order[first + i]] - (me[0] - 1) * leaves
         ok = (j < leaves) | (j >= 2 * leaves)
         slot = jnp.where(ok, jnp.where(j < leaves, j, j - leaves), 0)
         return ok, slot, counts[jnp.where(ok, j, 0)]
@@ -311,19 +334,19 @@
     return (joined(total) if across else total) * (SLOPE / 64)
 
 
-class Strided:
-    def __init__(self, array):
-        self.array = array
+class Relative:
+    def __init__(self, array, me):
+        self.array, self.me = array, me
 
     def __getitem__(self, n):
-        return self.array[n * COPIES]
+        return self.array[n ^ self.me]
 
 
 def upper_levels(coarse, me, box8, roots, c, fbs, fbt, pm, qm):
     def prep(t, carry):
         for s in range(8):
             b = 8 * t + s
-            fbs[b], fbt[b] = features(box8[b], c, True, True)
+            fbs[b], fbt[b] = features(twice(rows_of(box8, b, 0.0)), c, True, True)
         return carry
 
     lax.fori_loop(0, 7, prep, 0)
@@ -343,7 +366,7 @@
 
         lax.fori_loop(0, count // 8, body, 0)
 
-    merge(0, 32, Strided(roots), pm, 16)
+    merge(0, 32, Relative(roots, me), pm, 16)
     merge(32, 48, pm, qm, 8)
     n = me
     m = n >> 1
@@ -352,7 +375,7 @@
     def far(base, row, moments):
         target = fbt[row].astype(BF16)[:, :64]
         return far_sum(
-            lambda e: coarse[row, e], 16, lambda b: fbs[base + b], lambda b: moments[b], target, False
+            lambda e: coarse[e, row], 16, lambda b: fbs[base + b], lambda b: moments[b], target, False
         )
 
     def down(local, source, target):
@@ -361,24 +384,26 @@
 
     quad = far(48, 48 + t, qm)
     pair = down(quad, 48 + t, 32 + m) + far(32, 32 + m, pm)
-    return down(pair, 32 + m, n) + far(0, n, Strided(roots))
+    return down(pair, 32 + m, n) + far(0, n, Relative(roots, me))
 
 
 def far_kernel(
-    far, coarse, counts, me, own, pay_own, pay_low, pay_high, box8, roots, center,
-    out,
-    fps, fpt, mps, fbs, fbt, pm, qm, local,
-    *, leaves, factor,
+    far, coarse, me, own, low, high, box8, *rest, leaves, factor
 ):
-    c = center[:, 0:1]
+    *parts, out, fps, fpt, mps, fbs, fbt, pm, qm, local, roots = rest
+    roots[0] = parts[0][0]
+    for part in parts[1:]:
+        count = part.shape[0]
+        roots[count : 2 * count] = part[...]
+    c = center_of(own)
 
     def prep_far(t, carry):
         for s in range(4):
             i = t * 4 + s
-            for k, page in enumerate((pay_low, pay_own, pay_high)):
-                (fps[k * leaves + i],) = features(page[i, 8:16], c, True, False)
-                mps[k * leaves + i] = page[i, 0:8]
-            (fpt[i],) = features(pay_own[i, 8:16], c, False, True)
+            for k, (page, at) in enumerate(((low, 0), (own, 64), (high, 0))):
+                (fps[k * leaves + i],) = features(page[i, at + 8 : at + 16], c, True, False)
+                mps[k * leaves + i] = page[i, at : at + 8]
+            (fpt[i],) = features(own[i, 72:80], c, False, True)
         return carry
 
     lax.fori_loop(0, leaves // 4, prep_far, 0)
@@ -412,7 +437,7 @@
         for s in range(8):
             i = t * 8 + s
             source = fps[leaves + i].astype(BF16)[:, :64]
-            (points,) = features(own[i, 8:16], c, False, True)
+            (points,) = features(lanes_of(own, i, 8), c, False, True)
             basis = value_of(dot(source, points.astype(BF16), CN))
             out[i] = exact_dot(local[i], basis, NN) * factor
         return carry
@@ -441,54 +466,45 @@
     return pl.CostEstimate(flops=flops, transcendentals=0, bytes_accessed=1 << 20)
 
 
-def wide(array):
-    rows = jnp.concatenate([array, array], axis=2)
-    return jnp.pad(rows, ((0, 0), (0, 8 - array.shape[1]), (0, 0)))
-
-
 def local(points, probes, counts, near_list, far_list, coarse_list, leaf_proxy, box_proxy):
     leaves = points.shape[0]
     size = points.shape[2]
     nodes = lax.axis_size("space")
     device = lax.axis_index("space")
     factor = size ** (-0.5)
-    slot = lax.broadcasted_iota(jnp.int32, (leaves, 1, size), 2)
-    masked = jnp.where(slot < counts[:, None, None], probes, 0.0)
-    count_row = jnp.broadcast_to(counts.astype(F32)[:, None, None], (leaves, 5, size))
-    payload = jnp.concatenate([masked, points, count_row], axis=1)
+    half = lax.axis_index("probe") & 1
+    me = jnp.stack([device, half]).astype(jnp.int32)
+    points = jnp.transpose(points, (1, 0, 2))
+    leafp = jnp.transpose(leaf_proxy, (1, 0, 2))
+    boxp = jnp.transpose(box_proxy, (1, 0, 2))
+    near = near_list.T
     forward = [(i, i + 1) for i in range(nodes - 1)]
     backward = [(i + 1, i) for i in range(nodes - 1)]
     pairs = [(i, i ^ 1) for i in range(lax.axis_size("probe"))]
     partner = lax.ppermute(probes, "probe", pairs)
-    low = lax.ppermute(payload, "space", forward)
-    high = lax.ppermute(payload, "space", backward)
-    partner_low = lax.ppermute(partner, "space", forward)
-    partner_high = lax.ppermute(partner, "space", backward)
-    leafp = wide(leaf_proxy)
-    box8 = wide(box_proxy)
-    center = jnp.broadcast_to(jnp.pad(points[0, :, 0], (0, 5))[:, None], (8, 128))
-    own = lax.dynamic_index_in_dim(box8, device, 0, keepdims=False)
-    half = lax.axis_index("probe") & 1
-    me = jnp.stack([device, half]).astype(jnp.int32)
     params = pltpu.CompilerParams(vmem_limit_bytes=56 << 20)
     vm = pltpu.VMEM
     vmem = pl.BlockSpec(memory_space=vm)
     smem = pl.BlockSpec(memory_space=pltpu.SMEM)
     shape = jax.ShapeDtypeStruct
-    pay2, dev = pl.pallas_call(
+    page, dev = pl.pallas_call(
         functools.partial(moments_kernel, leaves=leaves, factor=factor),
-        out_shape=(shape((leaves, 16, 128), F32), shape((8, 128), F32)),
-        in_specs=[vmem] * 4,
+        out_shape=(shape((leaves, 80, 128), F32), shape((8, 128), F32)),
+        in_specs=[smem] * 2 + [vmem] * 4,
         out_specs=(vmem, vmem),
         scratch_shapes=[vm((leaves, FEATURES, 128), F32)],
         compiler_params=params,
         cost_estimate=cost(8),
         name="moments",
-    )(payload, leafp, own, center)
-    low2 = lax.ppermute(pay2, "space", forward)
-    high2 = lax.ppermute(pay2, "space", backward)
-    copies = jnp.broadcast_to(dev[None], (COPIES, 8, 128))
-    roots = lax.all_gather(copies, "space", axis=0, tiled=True)
+    )(counts, me, probes, points, leafp, boxp)
+    low = lax.ppermute(page, "space", forward)
+    high = lax.ppermute(page, "space", backward)
+    parts = [dev[None]]
+    for bit in range(nodes.bit_length() - 1):
+        swap = [(i, i ^ (1 << bit)) for i in range(nodes)]
+        parts.append(lax.ppermute(jnp.concatenate(parts, axis=0), "space", swap))
+    partner_low = lax.ppermute(partner, "space", forward)
+    partner_high = lax.ppermute(partner, "space", backward)
     targets = leaves // 2
 
     def work(blocks):
@@ -504,36 +520,40 @@
             + [vm((256, 256), F32)] * UNITS
         )
 
+    page, *parts = lax.optimization_barrier((page, *parts))
     acc0 = pl.pallas_call(
         functools.partial(own_kernel, leaves=leaves, targets=targets),
         out_shape=shape((targets * 2, 32, 256), F32),
-        in_specs=[smem] * 3 + [vmem] * 3,
+        in_specs=[smem] * 3 + [vmem] * 2,
         out_specs=vmem,
         scratch_shapes=work(leaves * 4 + 1),
         compiler_params=params,
         cost_estimate=cost(28),
         name="near_own",
-    )(near_list, counts, me, payload, partner, center)
-    low, high, low2, high2 = lax.optimization_barrier((low, high, low2, high2))
+    )(near, counts, me, page, partner)
     counts3 = jnp.concatenate(
         [low[:, 11, 0].astype(jnp.int32), counts, high[:, 11, 0].astype(jnp.int32)]
     )
     mine, theirs = pl.pallas_call(
         functools.partial(halo_kernel, leaves=leaves, targets=targets, factor=factor),
         out_shape=(shape((targets, 8, size), F32),) * 2,
-        in_specs=[smem] * 3 + [vmem] * 7,
+        in_specs=[smem] * 3 + [vmem] * 6,
         out_specs=(vmem, vmem),
         scratch_shapes=[vm((targets * 2, 32, 256), F32)] + work(2 * leaves * 4 + 1),
         compiler_params=params,
         cost_estimate=cost(30),
         name="near_halo",
-    )(near_list, counts3, me, payload, low, high, partner_low, partner_high, center, acc0)
+    )(near, counts3, me, page, low, high, partner_low, partner_high, acc0)
     back = lax.ppermute(theirs, "probe", pairs)
+    whole = lambda dims: pl.BlockSpec(dims, lambda i: (0,) * len(dims))
+    tail = pl.BlockSpec((leaves, 16, 128), lambda i: (0, 4, 0))
     far = pl.pallas_call(
         functools.partial(far_kernel, leaves=leaves, factor=factor),
         out_shape=shape(probes.shape, F32),
-        in_specs=[smem] * 4 + [vmem] * 7,
-        out_specs=vmem,
+        grid=(1,),
+        in_specs=[smem] * 3 + [whole(page.shape), tail, tail, whole(boxp.shape)]
+        + [whole(part.shape) for part in parts],
+        out_specs=whole(probes.shape),
         scratch_shapes=[
             vm((3 * leaves, FEATURES, 128), F32),
             vm((leaves, FEATURES, 128), F32),
@@ -543,11 +563,12 @@
             vm((nodes // 2, 8, 128), F32),
             vm((nodes // 4, 8, 128), F32),
             vm((leaves, 8, 64), F32),
+            vm((nodes, 8, 128), F32),
         ],
         compiler_params=params,
         cost_estimate=cost(30),
         name="far",
-    )(far_list, coarse_list, counts, me, payload, pay2, low2, high2, box8, roots, center)
+    )(far_list, coarse_list.T, me, page, low, high, boxp, *parts)
     return pl.pallas_call(
         functools.partial(sum_kernel, leaves=leaves),
         out_shape=shape(probes.shape, F32),

time: 155 us -> 145 us (0.935)
  between operations: 13.6 us -> 0.18 us
  waiting for transfers between devices: 0.04 us -> 8.54 us
  Pallas kernels: 99.9 us -> 106 us
  local copies, waits for them, and re-layouts: 9.1 us -> 3.02 us
  starting transfers between devices: 24.1 us -> 21.7 us
    ppermute x4 -> x7, waiting for transfers between devices: 0.01 us -> 8.53 us  [the longest x5 8.53 us: local(): parts.append(lax.ppermute(jnp.concatenate(parts, axis=0), 'space', swap))]
    pallas_call x1, Pallas kernels: 23.9 us -> 27.8 us  [local(): pl.pallas_call(functools.partial(own_kernel, leaves=leaves, targets=targe...]
    unnamed x33 -> x28, local copies, waits for them, and re-layouts: 5.59 us -> 3.02 us
    pallas_call x1, Pallas kernels: 30.7 us -> 32.8 us  [local(): pl.pallas_call(functools.partial(halo_kernel, leaves=leaves, targets=targ...]
    broadcast_in_dim x3 -> x0, local copies, waits for them, and re-layouts: 2.03 us -> none  [the longest x1 1.27 us: local(): copies = jnp.broadcast_to(dev[None], (COPIES, 8, 128))]
    ppermute x4 -> x7, starting transfers between devices: 12 us -> 11.6 us  [the longest x5 7.26 us: local(): parts.append(lax.ppermute(jnp.concatenate(parts, axis=0), 'space', swap))]
  transfers between devices with their start and end apart: 9 -> 11, of which waited for: 0 -> 4; matrix products, arithmetic and copies ran while one was open for 8% -> 4% of each run, Pallas kernels for 64% -> 49%
where the time goes in v1:
time: 145 us; the launch traced here: 144 us
  Pallas kernels  106 us (73%)
  starting transfers between devices  21.7 us (15%)
  waiting for transfers between devices  8.54 us (6%)
  other arithmetic  4.64 us (3%)
  local copies, waits for them, and re-layouts  3.02 us (2%)
    pallas_call x1, Pallas kernels, local(): pl.pallas_call(functools.partial(far_kernel, leaves=leaves, factor=factor...  33.8 us
    pallas_call x1, Pallas kernels, local(): pl.pallas_call(functools.partial(halo_kernel, leaves=leaves, targets=targ...  32.8 us
    pallas_call x1, Pallas kernels, local(): pl.pallas_call(functools.partial(own_kernel, leaves=leaves, targets=targe...  27.8 us
    ppermute x5, waiting for transfers between devices, local(): parts.append(lax.ppermute(jnp.concatenate(parts, axis=0), 'space', swap))  8.53 us
    pallas_call x1, Pallas kernels, local(): pl.pallas_call(functools.partial(moments_kernel, leaves=leaves, factor=fa...  8.39 us
    ppermute x5, starting transfers between devices, local(): parts.append(lax.ppermute(jnp.concatenate(parts, axis=0), 'space', swap))  7.26 us
    ppermute x1, starting transfers between devices, local(): partner_high = lax.ppermute(partner, 'space', backward)  5.27 us
    unnamed x28, local copies, waits for them, and re-layouts  3.02 us
  transfers between devices with their start and end apart: 11, of which 4 were waited for; matrix products, arithmetic and copies ran while one was open for 4% of the time, Pallas kernels for 49%

profile of v1, /device:TPU:8, one launch (start us, length us, event | category | flops | bytes accessed | tf_op | source)
XLA Modules:
  0.0 143.6 jit_solution(7784364999937621385)
XLA Ops:
  0.0 1.9 %collective-permute-start.7 = (f32[32,8,512]{2,1,0:T(8,128)}, f32[32,8,512]{2,1,0:T(8,128)S(1)}, u32[]{:S(2)}, u32[]{:S(2)}) collective-permute-start(f32[32,8,512]{2,1,0:T(8,128)} %probes.1), channel_id=1, source_target_pairs={{0,1},{1,0},{2,3},{3,2},{4,5},{5,4},{6,7},{7,6},{8,9},{9,8},{10,11... | collective-permute-start | bytes 1572872 | tf_op jit(solution)/shard_map/ppermute | solution.py:484
  1.9 0.7 pad_add_fusion.me
  2.6 8.4 %moments.1 = (f32[32,80,128]{2,1,0:T(8,128)}, f32[8,128]{1,0:T(8,128)}) custom-call(s32[32]{0:T(128)} %counts.5, s32[2]{0:T(128)} %pad_add_fusion.me, f32[32,8,512]{2,1,0:T(8,128)} %probes.1, f32[3,32,512]{2,1,0:T(8,128)} %bitcast.14, f32[3,32,64]{2,1,0:T(8,128)} %bitcast.17, f32[3,56,64]{2,1,0:T(8,128)} %bitcast.15), custom_call_target="tpu_custom_call" | custom-call | flops 8800000000 | bytes 1048576 | tf_op jit(solution)/shard_map/moments/pallas_call | solution.py:490
  11.0 0.0 collective-permute-start
  11.0 0.7 constant_dynamic-update-slice_fusion.4
  11.7 0.7 collective-permute-done.rest_1_
  12.3 0.0 copy-start.3
  12.4 0.7 pad_maximum_fusion.2
  13.0 1.5 %collective-permute-start.1 = (f32[2,8,128]{2,1,0:T(8,128)S(1)}, f32[2,8,128]{2,1,0:T(8,128)S(1)}, u32[]{:S(2)}, u32[]{:S(2)}) collective-permute-start(f32[2,8,128]{2,1,0:T(8,128)S(1)} %pad_maximum_fusion.2), channel_id=1, source_target_pairs={{0,8},{4,12},{8,0},{12,4},{16,24},{20,28},{24,16},{28,20},{32,40},... | collective-permute-start | bytes 24584 | tf_op jit(solution)/shard_map/ppermute | solution.py:505
  14.5 2.2 %collective-permute-done.1.rest_2_ = f32[2,8,128]{2,1,0:T(8,128)S(1)} collective-permute-done((f32[2,8,128]{2,1,0:T(8,128)S(1)}, f32[2,8,128]{2,1,0:T(8,128)S(1)}, u32[]{:S(2)}, u32[]{:S(2)}) %collective-permute-start.1) | collective-permute-done | bytes 8224 | tf_op jit(solution)/shard_map/ppermute | solution.py:505
  16.7 0.0 copy-start.1
  16.7 0.7 pad_maximum_fusion.1
  17.4 3.0 %collective-permute-start.2 = (f32[4,8,128]{2,1,0:T(8,128)S(1)}, f32[4,8,128]{2,1,0:T(8,128)S(1)}, u32[]{:S(2)}, u32[]{:S(2)}) collective-permute-start(f32[4,8,128]{2,1,0:T(8,128)S(1)} %pad_maximum_fusion.1), channel_id=1, source_target_pairs={{0,16},{4,20},{8,24},{12,28},{16,0},{20,4},{24,8},{28,12},{32,48},... | collective-permute-start | bytes 49160 | tf_op jit(solution)/shard_map/ppermute | solution.py:505
  20.4 2.2 %collective-permute-done.2.rest_3_ = f32[4,8,128]{2,1,0:T(8,128)S(1)} collective-permute-done((f32[4,8,128]{2,1,0:T(8,128)S(1)}, f32[4,8,128]{2,1,0:T(8,128)S(1)}, u32[]{:S(2)}, u32[]{:S(2)}) %collective-permute-start.2) | collective-permute-done | bytes 16416 | tf_op jit(solution)/shard_map/ppermute | solution.py:505
  22.6 0.0 copy-start.2
  22.6 0.7 pad_maximum_fusion
  23.3 0.5 collective-permute-start.3
  23.8 3.5 %collective-permute-done.3.rest_4_ = f32[8,8,128]{2,1,0:T(8,128)S(1)} collective-permute-done((f32[8,8,128]{2,1,0:T(8,128)S(1)}, f32[8,8,128]{2,1,0:T(8,128)S(1)}, u32[]{:S(2)}, u32[]{:S(2)}) %collective-permute-start.3) | collective-permute-done | bytes 32800 | tf_op jit(solution)/shard_map/ppermute | solution.py:505
  27.2 0.0 copy-start.4
  27.2 2.3 %collective-permute-start.4 = (f32[16,8,128]{2,1,0:T(8,128)S(1)}, f32[16,8,128]{2,1,0:T(8,128)S(1)}, u32[]{:S(2)}, u32[]{:S(2)}) collective-permute-start(f32[16,8,128]{2,1,0:T(8,128)S(1)} %constant_dynamic-update-slice_fusion), channel_id=1, source_target_pairs={{0,64},{4,68},{8,72},{12,76},{16,80},{20,84},{24,88},{28,92},{32,9... | collective-permute-start | bytes 196616 | tf_op jit(solution)/shard_map/ppermute | solution.py:505
  29.5 1.9 %collective-permute-start.6 = (f32[32,80,128]{2,1,0:T(8,128)}, f32[32,80,128]{2,1,0:T(8,128)S(1)}, u32[]{:S(2)}, u32[]{:S(2)}) collective-permute-start(f32[32,80,128]{2,1,0:T(8,128)} %get-tuple-element.18.own.page), channel_id=1, source_target_pairs={{4,0},{8,4},{12,8},{16,12},{20,16},{24,20},{28,24},{32,28},{36,32}... | collective-permute-start | bytes 3932168 | tf_op jit(solution)/shard_map/ppermute | solution.py:501
  31.5 2.4 %collective-permute-start.5 = (f32[32,80,128]{2,1,0:T(8,128)}, f32[32,80,128]{2,1,0:T(8,128)S(1)}, u32[]{:S(2)}, u32[]{:S(2)}) collective-permute-start(f32[32,80,128]{2,1,0:T(8,128)} %get-tuple-element.18.own.page), channel_id=1, source_target_pairs={{0,4},{4,8},{8,12},{12,16},{16,20},{20,24},{24,28},{28,32},{32,36}... | collective-permute-start | bytes 3932168 | tf_op jit(solution)/shard_map/ppermute | solution.py:500
  33.9 0.0 collective-permute-done.4.rest_5_
  33.9 0.0 copy-start.11
  33.9 0.0 collective-permute-done.7.partner
  33.9 0.0 copy-start.8
  33.9 5.3 %collective-permute-start.9 = (f32[32,8,512]{2,1,0:T(8,128)S(1)}, f32[32,8,512]{2,1,0:T(8,128)S(1)}, u32[]{:S(2)}, u32[]{:S(2)}) collective-permute-start(f32[32,8,512]{2,1,0:T(8,128)S(1)} %collective-permute-done.7.partner), channel_id=1, source_target_pairs={{4,0},{8,4},{12,8},{16,12},{20,16},{24,20},{28,24},{32,28},{36,32}... | collective-permute-start | bytes 1572872 | tf_op jit(solution)/shard_map/ppermute | solution.py:507
  39.2 1.9 %collective-permute-start.8 = (f32[32,8,512]{2,1,0:T(8,128)S(1)}, f32[32,8,512]{2,1,0:T(8,128)S(1)}, u32[]{:S(2)}, u32[]{:S(2)}) collective-permute-start(f32[32,8,512]{2,1,0:T(8,128)S(1)} %collective-permute-done.7.partner), channel_id=1, source_target_pairs={{0,4},{4,8},{8,12},{12,16},{16,20},{20,24},{24,28},{28,32},{32,36}... | collective-permute-start | bytes 1572872 | tf_op jit(solution)/shard_map/ppermute | solution.py:506
  41.1 0.0 copy-done.8
  41.1 0.0 copy-start.5
  41.1 27.8 %near_own.1.acc0 = f32[32,32,256]{2,1,0:T(8,128)} custom-call(s32[8,32]{1,0:T(8,128)} %bitcast.19, s32[32]{0:T(128)} %counts.5, s32[2]{0:T(128)} %pad_add_fusion.me, f32[32,80,128]{2,1,0:T(8,128)} %get-tuple-element.18.own.page, f32[32,8,512]{2,1,0:T(8,128)} %copy-done.8), custom_call_target="tpu_custom_call" | custom-call | flops 30799998976 | bytes 1048576 | tf_op jit(solution)/shard_map/near_own/pallas_call | solution.py:524
  68.9 0.0 copy-done.3
  68.9 0.0 copy-done.1
  68.9 0.0 copy-done.2
  68.9 0.0 copy-done.4
  68.9 0.0 copy-done.11
  68.9 0.0 collective-permute-done.6.high
  68.9 0.0 copy-start.6
  68.9 0.7 fusion
  69.6 0.0 collective-permute-done.5.low
  69.6 0.0 copy-start.7
  69.6 0.7 fusion.1
  70.3 0.0 copy-done.5
  70.3 0.6 pad_add_fusion.1.counts
  70.9 0.0 collective-permute-done.9.partner_high
  70.9 0.0 copy-start.9
  70.9 0.0 collective-permute-done.8.partner_low
  70.9 0.0 copy-done.6
  70.9 0.0 copy-done.7
  70.9 0.8 copy-done.9
  71.7 0.0 copy-start.10
  71.7 0.8 copy-done.10
  72.5 32.8 %near_halo.1 = (f32[16,8,512]{2,1,0:T(8,128)}, f32[16,8,512]{2,1,0:T(8,128)}) custom-call(s32[8,32]{1,0:T(8,128)} %bitcast.20, s32[96]{0:T(128)} %pad_add_fusion.1.counts, s32[2]{0:T(128)} %pad_add_fusion.me, f32[32,80,128]{2,1,0:T(8,128)} %get-tuple-element.18.own.page, f32[32,80,128]{2,1,0:T(8,128)} %copy-done.7, f32[32,80,128]{2,1,0:T(8,128)} %copy-done.6, ...), custom_call_target="tpu_custom_call" | custom-call | flops 32999999488 | bytes 1048576 | tf_op jit(solution)/shard_map/near_halo/pallas_call | solution.py:537
  105.3 1.0 collective-permute-start.10
  106.3 33.8 %far.2 = f32[32,8,512]{2,1,0:T(8,128)} custom-call(s32[32,32]{1,0:T(8,128)} %far.3, s32[16,56]{1,0:T(8,128)} %bitcast.18, s32[2]{0:T(128)} %pad_add_fusion.me, f32[32,80,128]{2,1,0:T(8,128)} %get-tuple-element.18.own.page, f32[32,80,128]{2,1,0:T(8,128)} %copy-done.7, f32[32,80,128]{2,1,0:T(8,128)} %copy-done.6, f32[3,56,64]{2,1,0:T(8,128)} %bitcast.16, ...), custom_call_target="tpu_custom_call" | custom-call | flops 32999999488 | bytes 1048576 | tf_op jit(solution)/shard_map/far/pallas_call | solution.py:550
  140.1 0.0 collective-permute-done.10.back
  140.1 0.0 copy-start
  140.1 0.7 copy-done
  140.8 2.8 %sum.1 = f32[32,8,512]{2,1,0:T(8,128)} custom-call(s32[32]{0:T(128)} %counts.5, s32[2]{0:T(128)} %pad_add_fusion.me, f32[32,8,512]{2,1,0:T(8,128)} %far.2, f32[16,8,512]{2,1,0:T(8,128)} %get-tuple-element.25.mine, f32[16,8,512]{2,1,0:T(8,128)} %copy-done), custom_call_target="tpu_custom_call" | custom-call | tf_op jit(solution)/shard_map/sum/pallas_call | solution.py:572
  (4 shorter events, 0.0 us)
Async XLA Ops:
  0.0 33.9 %collective-permute-start.7 = (f32[32,8,512]{2,1,0:T(8,128)}, f32[32,8,512]{2,1,0:T(8,128)S(1)}, u32[]{:S(2)}, u32[]{:S(2)}) collective-permute-start(f32[32,8,512]{2,1,0:T(8,128)} %probes.1), channel_id=1, source_target_pairs={{0,1},{1,0},{2,3},{3,2},{4,5},{5,4},{6,7},{7,6},{8,9},{9,8},{10,11... | collective-permute-start | bytes 1572872 | tf_op jit(solution)/shard_map/ppermute | solution.py:484
  11.0 1.4 collective-permute-start
  12.3 56.5 %copy-start.3 = (f32[1,8,128]{2,1,0:T(8,128)}, f32[1,8,128]{2,1,0:T(8,128)S(1)}, u32[]{:S(2)}) copy-start(f32[1,8,128]{2,1,0:T(8,128)S(1)} %collective-permute-done.rest_1_) | copy-start | bytes 12292
  13.0 3.7 %collective-permute-start.1 = (f32[2,8,128]{2,1,0:T(8,128)S(1)}, f32[2,8,128]{2,1,0:T(8,128)S(1)}, u32[]{:S(2)}, u32[]{:S(2)}) collective-permute-start(f32[2,8,128]{2,1,0:T(8,128)S(1)} %pad_maximum_fusion.2), channel_id=1, source_target_pairs={{0,8},{4,12},{8,0},{12,4},{16,24},{20,28},{24,16},{28,20},{32,40},... | collective-permute-start | bytes 24584 | tf_op jit(solution)/shard_map/ppermute | solution.py:505
  16.7 52.2 %copy-start.1 = (f32[2,8,128]{2,1,0:T(8,128)}, f32[2,8,128]{2,1,0:T(8,128)S(1)}, u32[]{:S(2)}) copy-start(f32[2,8,128]{2,1,0:T(8,128)S(1)} %collective-permute-done.1.rest_2_) | copy-start | bytes 24580
  17.4 5.2 %collective-permute-start.2 = (f32[4,8,128]{2,1,0:T(8,128)S(1)}, f32[4,8,128]{2,1,0:T(8,128)S(1)}, u32[]{:S(2)}, u32[]{:S(2)}) collective-permute-start(f32[4,8,128]{2,1,0:T(8,128)S(1)} %pad_maximum_fusion.1), channel_id=1, source_target_pairs={{0,16},{4,20},{8,24},{12,28},{16,0},{20,4},{24,8},{28,12},{32,48},... | collective-permute-start | bytes 49160 | tf_op jit(solution)/shard_map/ppermute | solution.py:505
  22.6 46.3 %copy-start.2 = (f32[4,8,128]{2,1,0:T(8,128)}, f32[4,8,128]{2,1,0:T(8,128)S(1)}, u32[]{:S(2)}) copy-start(f32[4,8,128]{2,1,0:T(8,128)S(1)} %collective-permute-done.2.rest_3_) | copy-start | bytes 49156
  23.3 3.9 %collective-permute-start.3 = (f32[8,8,128]{2,1,0:T(8,128)S(1)}, f32[8,8,128]{2,1,0:T(8,128)S(1)}, u32[]{:S(2)}, u32[]{:S(2)}) collective-permute-start(f32[8,8,128]{2,1,0:T(8,128)S(1)} %pad_maximum_fusion), channel_id=1, source_target_pairs={{0,32},{4,36},{8,40},{12,44},{16,48},{20,52},{24,56},{28,60},{32,0... | collective-permute-start | bytes 98312 | tf_op jit(solution)/shard_map/ppermute | solution.py:505
  27.2 41.7 %copy-start.4 = (f32[8,8,128]{2,1,0:T(8,128)}, f32[8,8,128]{2,1,0:T(8,128)S(1)}, u32[]{:S(2)}) copy-start(f32[8,8,128]{2,1,0:T(8,128)S(1)} %collective-permute-done.3.rest_4_) | copy-start | bytes 98308
  27.2 6.6 %collective-permute-start.4 = (f32[16,8,128]{2,1,0:T(8,128)S(1)}, f32[16,8,128]{2,1,0:T(8,128)S(1)}, u32[]{:S(2)}, u32[]{:S(2)}) collective-permute-start(f32[16,8,128]{2,1,0:T(8,128)S(1)} %constant_dynamic-update-slice_fusion), channel_id=1, source_target_pairs={{0,64},{4,68},{8,72},{12,76},{16,80},{20,84},{24,88},{28,92},{32,9... | collective-permute-start | bytes 196616 | tf_op jit(solution)/shard_map/ppermute | solution.py:505
  29.5 39.4 %collective-permute-start.6 = (f32[32,80,128]{2,1,0:T(8,128)}, f32[32,80,128]{2,1,0:T(8,128)S(1)}, u32[]{:S(2)}, u32[]{:S(2)}) collective-permute-start(f32[32,80,128]{2,1,0:T(8,128)} %get-tuple-element.18.own.page), channel_id=1, source_target_pairs={{4,0},{8,4},{12,8},{16,12},{20,16},{24,20},{28,24},{32,28},{36,32}... | collective-permute-start | bytes 3932168 | tf_op jit(solution)/shard_map/ppermute | solution.py:501
  31.5 38.2 %collective-permute-start.5 = (f32[32,80,128]{2,1,0:T(8,128)}, f32[32,80,128]{2,1,0:T(8,128)S(1)}, u32[]{:S(2)}, u32[]{:S(2)}) collective-permute-start(f32[32,80,128]{2,1,0:T(8,128)} %get-tuple-element.18.own.page), channel_id=1, source_target_pairs={{0,4},{4,8},{8,12},{12,16},{16,20},{20,24},{24,28},{28,32},{32,36}... | collective-permute-start | bytes 3932168 | tf_op jit(solution)/shard_map/ppermute | solution.py:500
  33.9 35.0 %copy-start.11 = (f32[16,8,128]{2,1,0:T(8,128)}, f32[16,8,128]{2,1,0:T(8,128)S(1)}, u32[]{:S(2)}) copy-start(f32[16,8,128]{2,1,0:T(8,128)S(1)} %collective-permute-done.4.rest_5_) | copy-start | bytes 196612
  33.9 7.2 %copy-start.8 = (f32[32,8,512]{2,1,0:T(8,128)}, f32[32,8,512]{2,1,0:T(8,128)S(1)}, u32[]{:S(2)}) copy-start(f32[32,8,512]{2,1,0:T(8,128)S(1)} %collective-permute-done.7.partner) | copy-start | bytes 1572868
  33.9 37.0 %collective-permute-start.9 = (f32[32,8,512]{2,1,0:T(8,128)S(1)}, f32[32,8,512]{2,1,0:T(8,128)S(1)}, u32[]{:S(2)}, u32[]{:S(2)}) collective-permute-start(f32[32,8,512]{2,1,0:T(8,128)S(1)} %collective-permute-done.7.partner), channel_id=1, source_target_pairs={{4,0},{8,4},{12,8},{16,12},{20,16},{24,20},{28,24},{32,28},{36,32}... | collective-permute-start | bytes 1572872 | tf_op jit(solution)/shard_map/ppermute | solution.py:507
  39.2 31.7 %collective-permute-start.8 = (f32[32,8,512]{2,1,0:T(8,128)S(1)}, f32[32,8,512]{2,1,0:T(8,128)S(1)}, u32[]{:S(2)}, u32[]{:S(2)}) collective-permute-start(f32[32,8,512]{2,1,0:T(8,128)S(1)} %collective-permute-done.7.partner), channel_id=1, source_target_pairs={{0,4},{4,8},{8,12},{12,16},{16,20},{20,24},{24,28},{28,32},{32,36}... | collective-permute-start | bytes 1572872 | tf_op jit(solution)/shard_map/ppermute | solution.py:506
  41.1 29.2 %copy-start.5 = (s32[32]{0:T(128)S(1)}, s32[32]{0:T(128)}, u32[]{:S(2)}) copy-start(s32[32]{0:T(128)} %counts.5) | copy-start | bytes 388
  68.9 2.0 %copy-start.6 = (f32[32,80,128]{2,1,0:T(8,128)}, f32[32,80,128]{2,1,0:T(8,128)S(1)}, u32[]{:S(2)}) copy-start(f32[32,80,128]{2,1,0:T(8,128)S(1)} %collective-permute-done.6.high) | copy-start | bytes 3932164
  69.6 1.3 copy-start.7
  70.9 0.8 copy-start.9
  71.7 0.8 copy-start.10
  105.3 34.8 %collective-permute-start.10 = (f32[16,8,512]{2,1,0:T(8,128)}, f32[16,8,512]{2,1,0:T(8,128)S(1)}, u32[]{:S(2)}, u32[]{:S(2)}) collective-permute-start(f32[16,8,512]{2,1,0:T(8,128)} %get-tuple-element.26), channel_id=1, source_target_pairs={{0,1},{1,0},{2,3},{3,2},{4,5},{5,4},{6,7},{7,6},{8,9},{9,8},{10,11... | collective-permute-start | bytes 786440 | tf_op jit(solution)/shard_map/ppermute | solution.py:547
  140.1 0.7 copy-start
